TPU v7x, 32 devices: a whole 2x2x4 slice. The times are simulated.
32 devices in a mesh: tile: 8 (over z, x), tp: 4 (over y, core).
Axes of the slice: x: 2, y: 2, z: 4, core: 2. Of those that a mesh axis runs over, the one named last changes fastest.
Arguments:
- latent: bfloat16 [512, 1024], P(('tile', 'tp')), may hold values from -6 to 6
- weight_in: bfloat16 [1024, 4096], P(None, 'tp'), may hold values from -0.1875 to 0.1875
- weight_out: bfloat16 [4096, 1024], P('tp'), may hold values from -0.09375 to 0.09375
- weight_conv: bfloat16 [7168, 2048], P(None, 'tp'), may hold values from -0.0625 to 0.0625
- neighbours: int32 [512, 7], P('tile'), may hold values from 0 to 96, as said below
- child_order: int32 [2048], P(('tile', 'tp')), may hold values from 0 to 63, as said below
- cotangent: bfloat16 [2048, 512], P(('tile', 'tp')), may hold values from -6 to 6
Outputs:
- fine_cells: bfloat16 [2048, 512], P(('tile', 'tp'))
- grad_latent: float32 [512, 1024], P(('tile', 'tp'))
- weight_in_grad: float32 [1024, 4096], P('tile', 'tp')
- weight_out_grad: float32 [4096, 1024], P('tp', 'tile')
- weight_conv_grad: float32 [7168, 2048], P('tile', 'tp')
Inputs may be any that keep to these rules, and one draw needn't show every extreme that they name: `neighbours`: column 0 of the row of a tile's i-th cell is i + 16 (the cell itself); the other columns lie within 16 of it, except that index 96, the empty row, marks a missing sixth neighbour of a pentagon cell. `child_order`: each block of 64 consecutive entries is a permutation of 0 .. 63.
All inputs are finite; a program needn't handle non-finite values.
Results may differ from a plain program's by a relative error of at most 0.02.
Values may be sent and summed in bfloat16 or wider, within the bound.
No kernel may reach another device: no remote copies, remote signals or barrier semaphores. Data moves between devices by JAX's collectives and lax.ppermute only.
A program may use at most 128 MiB of HBM per device.

v0:
```python
import math
import jax
import jax.numpy as jnp
from jax import lax
from jax.sharding import PartitionSpec as P

SLOTS = 4
HALO = 16
EPSILON = 1e-05


def with_halo(value, sides, width):
    for axis, dim in sides:
        count, length = (lax.axis_size(axis), value.shape[dim])
        up = [(i, (i + 1) % count) for i in range(count - 1)]
        down = [(j, i) for i, j in up]
        last = lax.slice_in_dim(value, length - width, length, axis=dim)
        initial = lax.slice_in_dim(value, 0, width, axis=dim)
        before = lax.ppermute(last, axis, up)
        after = lax.ppermute(initial, axis, down)
        value = jnp.concatenate([before, value, after], axis=dim)
    return value


def silu_grad(pre_value):
    sigmoid = jax.nn.sigmoid(pre_value)
    return sigmoid * (1.0 + pre_value * (1.0 - sigmoid))


def tp_rows(pieces):
    return lax.all_gather(pieces, "tp", axis=0, tiled=True)


def tp_sums(terms):
    return lax.psum(terms.astype(jnp.bfloat16), "tp").astype(jnp.float32)


def tile_margin(tile_data):
    return with_halo(tile_data, (("tile", 0),), HALO)


def regroup(block_data):
    return lax.all_to_all(block_data, "tp", split_axis=0, concat_axis=0, tiled=True)


def local(latent, weight_in, weight_out, weight_conv, neighbours, child_order, cotangent):
    groups = lax.axis_size("tp")
    tiles = lax.axis_size("tile")
    sub_rows = latent.shape[0]
    features = latent.shape[1]
    tile_rows = sub_rows * groups
    grad_scale = 1.0 / math.sqrt(tile_rows * tiles)
    tap_count = neighbours.shape[1]
    shard_cols = weight_conv.shape[1]
    shard_chans = shard_cols // SLOTS
    own_start = lax.axis_index("tp") * sub_rows
    source = latent.astype(jnp.float32)
    whole_source = tp_rows(latent).astype(jnp.float32)
    tile_norm = lax.rsqrt(jnp.mean(whole_source * whole_source, axis=1, keepdims=True) + EPSILON)
    norm_factor = lax.dynamic_slice_in_dim(tile_norm, own_start, sub_rows, 0)
    normed = (whole_source * tile_norm).astype(jnp.bfloat16)
    pre_act = jnp.dot(normed, weight_in, preferred_element_type=jnp.float32)
    hidden = jax.nn.silu(pre_act).astype(jnp.bfloat16)
    mixed = tp_sums(jnp.dot(hidden, weight_out, preferred_element_type=jnp.float32))
    latent_tile = (whole_source + mixed).astype(jnp.bfloat16)
    extended = jnp.concatenate(
        [tile_margin(latent_tile), jnp.zeros((1, features), jnp.bfloat16)], axis=0
    )
    tap_rows = jnp.take(extended, neighbours, axis=0).reshape(tile_rows, tap_count * features)
    coarse_out = jnp.dot(tap_rows, weight_conv, preferred_element_type=jnp.float32).astype(
        jnp.bfloat16
    )
    own_blocks = regroup(coarse_out)
    children = own_blocks.reshape(groups, sub_rows, shard_chans, SLOTS).transpose(1, 3, 0, 2)
    children = children.reshape(sub_rows * SLOTS, groups * shard_chans)
    activated = jax.nn.silu(children.astype(jnp.float32)).astype(jnp.bfloat16)
    fine_cells = jnp.take(activated, child_order, axis=0)
    child_grad = jnp.zeros_like(cotangent).at[child_order].set(cotangent)
    child_pre_grad = (
        child_grad.astype(jnp.float32) * silu_grad(children.astype(jnp.float32))
    ).astype(jnp.bfloat16)
    outgoing = child_pre_grad.reshape(sub_rows, SLOTS, groups, shard_chans).transpose(2, 0, 3, 1)
    coarse_grad = regroup(outgoing.reshape(groups * sub_rows, shard_cols))
    weight_conv_grad = lax.psum_scatter(
        (
            jnp.einsum("rk,rc->kc", tap_rows, coarse_grad, preferred_element_type=jnp.float32)
            * grad_scale
        ).astype(jnp.bfloat16),
        "tile",
        scatter_dimension=0,
        tiled=True,
    ).astype(jnp.float32)
    tap_grad = jnp.dot(coarse_grad, weight_conv.T, preferred_element_type=jnp.float32)
    tap_grad = tap_grad.reshape(tile_rows * tap_count, features)
    ext_grad = (
        jnp.zeros((tile_rows + 2 * HALO + 1, features), jnp.float32)
        .at[neighbours.reshape(-1)]
        .add(tap_grad)
    )
    rim_rows = jnp.concatenate(
        [ext_grad[:HALO], ext_grad[tile_rows + HALO : tile_rows + 2 * HALO]], axis=0
    ).astype(jnp.bfloat16)
    arrived = tile_margin(rim_rows).astype(jnp.float32)
    partial_value = ext_grad[HALO : HALO + tile_rows]
    partial_value = partial_value.at[:HALO].add(arrived[:HALO])
    partial_value = partial_value.at[tile_rows - HALO :].add(arrived[3 * HALO :])
    latent_grad = lax.psum_scatter(
        partial_value.astype(jnp.bfloat16), "tp", scatter_dimension=0, tiled=True
    ).astype(jnp.float32)
    upstream = tp_rows(latent_grad.astype(jnp.bfloat16))
    hidden_grad = jnp.dot(upstream, weight_out.T, preferred_element_type=jnp.float32)
    pre_grad = (hidden_grad * silu_grad(pre_act)).astype(jnp.bfloat16)
    out_term = (
        jnp.einsum("rf,rd->fd", hidden, upstream, preferred_element_type=jnp.float32) * grad_scale
    )
    weight_out_grad = lax.psum_scatter(
        out_term.astype(jnp.bfloat16), "tile", scatter_dimension=1, tiled=True
    ).astype(jnp.float32)
    normed_whole = tp_sums(jnp.dot(pre_grad, weight_in.T, preferred_element_type=jnp.float32))
    normed_grad = lax.dynamic_slice_in_dim(normed_whole, own_start, sub_rows, 0)
    grad_latent = (
        latent_grad
        + norm_factor * normed_grad
        - source
        * norm_factor
        * norm_factor
        * norm_factor
        * jnp.mean(normed_grad * source, axis=1, keepdims=True)
    )
    weight_in_grad = lax.psum_scatter(
        (
            jnp.einsum("rd,rf->df", normed, pre_grad, preferred_element_type=jnp.float32)
            * grad_scale
        ).astype(jnp.bfloat16),
        "tile",
        scatter_dimension=0,
        tiled=True,
    ).astype(jnp.float32)
    return (fine_cells, grad_latent, weight_in_grad, weight_out_grad, weight_conv_grad)


def solution(mesh):
    placed = (
        P(("tile", "tp"), None),
        P(None, "tp"),
        P("tp", None),
        P(None, "tp"),
        P("tile", None),
        P(("tile", "tp")),
        P(("tile", "tp"), None),
    )
    return jax.shard_map(
        local,
        mesh=mesh,
        in_specs=placed,
        out_specs=(
            P(("tile", "tp"), None),
            P(("tile", "tp"), None),
            P("tile", "tp"),
            P("tp", "tile"),
            P("tile", "tp"),
        ),
        check_vma=False,
    )
```

profile of v0, /device:TPU:0, one launch (start us, length us, event | category | flops | bytes accessed | tf_op | source)
XLA Modules:
  0.0 469.5 jit_solution(18033173362639526849)
XLA Ops:
  7.2 6.9 %all_gather.6 = bf16[64,1024]{1,0:T(8,128)(2,1)S(1)} all-gather(bf16[16,1024]{1,0:T(8,128)(2,1)} %param.11), channel_id=1, replica_groups=mesh['tile'=8,'tp'=4] {'tp'}, dimensions={0}, use_global_device_ids=true | all-gather | bytes 163840 | tf_op jit(solution)/shard_map/all_gather | solution.py:31
  14.1 0.1 fusion.1
  14.3 2.1 fusion.23
  16.4 1.1 convolution_convert_fusion.1
  17.6 0.1 copy.28
  17.7 0.1 reshape.168
  17.8 33.3 %all-reduce.3.cloned.1.call-done = bf16[64,1024]{1,0:T(8,128)(2,1)} async-done(((bf16[64,1024]{1,0:T(8,128)(2,1)}), bf16[64,1024]{1,0:T(8,128)(2,1)}) %all-reduce.3.cloned.1.call-update) | async-done | bytes 131088 | tf_op jit(solution)/shard_map/psum | solution.py:35
  51.1 0.9 fusion.3
  52.1 3.4 collective-permute-start
  55.4 1.3 collective-permute-start.1
  56.8 0.1 copy.27
  56.9 0.1 pad.11.clone
  56.9 0.1 collective-permute-done
  57.0 4.2 collective-permute-done.1
  61.3 0.1 maximum_maximum_fusion
  61.4 2.7 gather_fusion
  64.1 2.2 reshape.167
  66.3 1.4 broadcast_select_fusion
  67.7 0.6 copy.36
  68.3 5.1 %convolution_convert_fusion.2 = bf16[64,512]{1,0:T(8,128)(2,1)} fusion(bf16[64,7168]{1,0:T(8,128)(2,1)S(1)} %bitcast.55, bf16[7168,512]{1,0:T(8,128)(2,1)} %param.14), kind=kOutput, calls=%fused_computation.11 | convolution fusion | flops 469794816 | bytes 8323072 | tf_op jit(solution)/shard_map/dot_general | solution.py:70
  73.4 3.3 all-to-all-start
  76.7 0.1 copy.31
  76.8 0.1 reshape.161
  77.0 1.2 scatter_custom_fusion
  78.1 2.7 all-to-all-done
  80.8 1.2 copy.29
  82.0 1.5 copy.30
  83.5 0.1 fusion.13
  83.6 1.1 copy.32
  84.7 1.8 copy.33
  86.6 3.3 all-to-all-start.1
  89.9 4.0 all-to-all-done.1
  93.9 6.6 %fusion.29 = f32[64,7168]{1,0:T(8,128)} fusion(bf16[64,512]{1,0:T(8,128)(2,1)S(1)} %bitcast.61, bf16[7168,512]{1,0:T(8,128)(2,1)} %param.14), kind=kOutput, calls=%fused_computation.66 | convolution fusion | flops 469762048 | bytes 9240576 | tf_op jit(solution)/shard_map/dot_general | solution.py:93
  100.6 2.7 reshape.194
  103.3 5.8 %scatter_custom_fusion.1 = f32[97,1024]{1,0:T(8,128)} fusion(s32[448]{0:T(512)S(1)} %bitcast.65, f32[448,1024]{1,0:T(8,128)} %reshape.194, f32[]{:T(128)} %constant.110.clone.1), kind=kCustom, calls=%fused_computation.22 | custom fusion | flops 458752 | bytes 397824 | tf_op jit(solution)/shard_map/scatter-add | solution.py:98
  109.1 1.0 convert.9
  110.1 4.3 collective-permute-start.2
  114.4 1.3 collective-permute-start.3
  115.7 1.0 slice.79
  116.7 3.5 collective-permute-done.3
  120.2 0.8 fusion.21
  121.1 0.7 convert_element_type.99
  121.8 0.0 all-reduce.5.cloned.1.call-start
  121.8 18.8 %reduce-scatter.7.cloned.1.call-done = bf16[16,1024]{1,0:T(8,128)(2,1)} async-done(((bf16[64,1024]{1,0:T(8,128)(2,1)}), bf16[16,1024]{1,0:T(8,128)(2,1)}) %reduce-scatter.7.cloned.1.call-update) | async-done | bytes 32784 | tf_op jit(solution)/shard_map/reduce_scatter | solution.py:107
  140.7 5.9 %all_gather.7 = bf16[64,1024]{1,0:T(8,128)(2,1)S(1)} all-gather(bf16[16,1024]{1,0:T(8,128)(2,1)} %reduce-scatter.7.cloned.1.call-done), channel_id=1, replica_groups=mesh['tile'=8,'tp'=4] {'tp'}, dimensions={0}, use_global_device_ids=true | all-gather | bytes 163840 | tf_op jit(solution)/shard_map/all_gather | solution.py:31
  146.6 1.7 fusion
  148.3 1.4 convolution_convert_fusion
  149.8 3.1 multiply_convert_fusion.1
  152.9 4.0 copy.34
  156.9 2.1 multiply_convert_fusion.2
  159.1 5.1 %multiply_convert_fusion = bf16[7168,512]{1,0:T(8,128)(2,1)} fusion(bf16[64,7168]{1,0:T(8,128)(2,1)S(1)} %bitcast.56, bf16[64,512]{1,0:T(8,128)(2,1)S(1)} %bitcast.62), kind=kOutput, calls=%fused_computation.4 | convolution fusion | flops 477102080 | bytes 8323072 | tf_op jit(solution)/shard_map/rk,rc->kc/dot_general | solution.py:86
  164.2 0.1 dynamic-slice.19
  164.3 0.7 gather_fusion.1
  165.0 0.7 broadcast_select_fusion.1
  165.7 16.0 %all-reduce.5.cloned.1.call-done = bf16[64,1024]{1,0:T(8,128)(2,1)} async-done(((bf16[64,1024]{1,0:T(8,128)(2,1)}), bf16[64,1024]{1,0:T(8,128)(2,1)}) %all-reduce.5.cloned.1.call-update) | async-done | bytes 131088 | tf_op jit(solution)/shard_map/psum | solution.py:35
  181.7 0.9 fusion.19
  182.6 1.5 fusion.15
  184.1 69.7 %reduce-scatter.13.cloned.1.call-done = bf16[128,1024]{1,0:T(8,128)(2,1)} async-done(((bf16[1024,1024]{1,0:T(8,128)(2,1)}), bf16[128,1024]{1,0:T(8,128)(2,1)}) %reduce-scatter.13.cloned.1.call-update) | async-done | bytes 262160
  253.8 1.1 copy.35
  254.9 0.8 convert_element_type.108
  255.8 68.8 %reduce-scatter.9.cloned.1.call-done = bf16[128,1024]{1,0:T(8,128)(2,1)} async-done(((bf16[1024,1024]{1,0:T(8,128)(2,1)}), bf16[128,1024]{1,0:T(8,128)(2,1)}) %reduce-scatter.9.cloned.1.call-update) | async-done | bytes 262160 | tf_op jit(solution)/shard_map/reduce_scatter | solution.py:130
  324.6 1.8 convert_element_type.106
  326.4 133.6 %reduce-scatter.11.cloned.1.call-done = bf16[896,512]{1,0:T(8,128)(2,1)} async-done(((bf16[7168,512]{1,0:T(8,128)(2,1)}), bf16[896,512]{1,0:T(8,128)(2,1)}) %reduce-scatter.11.cloned.1.call-update) | async-done | bytes 917520 | tf_op jit(solution)/shard_map/reduce_scatter | solution.py:84
  460.0 2.7 convert_element_type.110
  (39 shorter events, 0.4 us)
Async XLA Ops:
  7.2 9.2 %copy-start = (bf16[1024,1024]{1,0:T(8,128)(2,1)S(1)}, bf16[1024,1024]{1,0:T(8,128)(2,1)}, u32[]{:S(2)}) copy-start(bf16[1024,1024]{1,0:T(8,128)(2,1)} %param.13) | copy-start | bytes 6291460
  7.2 43.9 %all-reduce.3.cloned.1.call-start = ((), (), s32[]{:S(2)}) async-start(), calls=%async_computation.6 | async-start | bytes 262144 | tf_op jit(solution)/shard_map/psum | solution.py:35
  14.2 3.3 copy-start.5
  16.4 1.4 copy-start.3
  52.1 5.0 %collective-permute-start = (bf16[16,1024]{1,0:T(8,128)(2,1)S(1)}, bf16[16,1024]{1,0:T(8,128)(2,1)S(1)}, u32[]{:S(2)}, u32[]{:S(2)}) collective-permute-start(bf16[16,1024]{1,0:T(8,128)(2,1)S(1)} %get-tuple-element.33), channel_id=1, source_target_pairs={{0,4},{4,8},{8,12},{12,16},{16,20},{20,24},{24,28},{1,5},{5,9},{9,... | collective-permute-start | bytes 98312 | tf_op jit(solution)/shard_map/ppermute | solution.py:19
  55.4 5.8 %collective-permute-start.1 = (bf16[16,1024]{1,0:T(8,128)(2,1)S(1)}, bf16[16,1024]{1,0:T(8,128)(2,1)S(1)}, u32[]{:S(2)}, u32[]{:S(2)}) collective-permute-start(bf16[16,1024]{1,0:T(8,128)(2,1)S(1)} %get-tuple-element.34), channel_id=1, source_target_pairs={{4,0},{8,4},{12,8},{16,12},{20,16},{24,20},{28,24},{5,1},{9,5},{13... | collective-permute-start | bytes 98312 | tf_op jit(solution)/shard_map/ppermute | solution.py:20
  68.3 8.4 %copy-start.6 = (s32[64]{0:T(128)S(1)}, s32[64]{0:T(128)}, u32[]{:S(2)}) copy-start(s32[64]{0:T(128)} %param.16) | copy-start | bytes 772
  73.4 7.4 %all-to-all-start = ((bf16[4,16,512]{2,1,0:T(8,128)(2,1)}), bf16[4,16,512]{2,1,0:T(8,128)(2,1)S(1)}, u32[]{:S(2)}, u32[]{:S(2)}) async-start(bf16[4,16,512]{2,1,0:T(8,128)(2,1)} %bitcast), calls=%async_computation | async-start | bytes 131072 | tf_op jit(solution)/shard_map/all_to_all | solution.py:43
  86.6 7.4 %all-to-all-start.1 = ((bf16[4,16,512]{2,1,0:T(8,128)(2,1)}), bf16[4,16,512]{2,1,0:T(8,128)(2,1)S(1)}, u32[]{:S(2)}, u32[]{:S(2)}) async-start(bf16[4,16,512]{2,1,0:T(8,128)(2,1)} %copy.33), calls=%async_computation.1 | async-start | bytes 131072 | tf_op jit(solution)/shard_map/all_to_all | solution.py:43
  89.9 50.8 %reduce-scatter.7.cloned.1.call-start = ((), (), s32[]{:S(2)}) async-start(), calls=%async_computation.7 | async-start | bytes 163840 | tf_op jit(solution)/shard_map/reduce_scatter | solution.py:107
  110.1 6.6 %collective-permute-start.2 = (bf16[16,1024]{1,0:T(8,128)(2,1)S(1)}, bf16[16,1024]{1,0:T(8,128)(2,1)S(1)}, u32[]{:S(2)}, u32[]{:S(2)}) collective-permute-start(bf16[16,1024]{1,0:T(8,128)(2,1)S(1)} %get-tuple-element.29), channel_id=1, source_target_pairs={{0,4},{4,8},{8,12},{12,16},{16,20},{20,24},{24,28},{1,5},{5,9},{9,... | collective-permute-start | bytes 98312 | tf_op jit(solution)/shard_map/ppermute | solution.py:19
  114.4 5.8 %collective-permute-start.3 = (bf16[16,1024]{1,0:T(8,128)(2,1)S(1)}, bf16[16,1024]{1,0:T(8,128)(2,1)S(1)}, u32[]{:S(2)}, u32[]{:S(2)}) collective-permute-start(bf16[16,1024]{1,0:T(8,128)(2,1)S(1)} %get-tuple-element.30), channel_id=1, source_target_pairs={{4,0},{8,4},{12,8},{16,12},{20,16},{24,20},{28,24},{5,1},{9,5},{13... | collective-permute-start | bytes 98312 | tf_op jit(solution)/shard_map/ppermute | solution.py:20
  121.8 59.9 %all-reduce.5.cloned.1.call-start = ((), (), s32[]{:S(2)}) async-start(), calls=%async_computation.8 | async-start | bytes 262144 | tf_op jit(solution)/shard_map/psum | solution.py:35
  140.7 7.6 %copy-start.1 = (bf16[1024,1024]{1,0:T(8,128)(2,1)S(1)}, bf16[1024,1024]{1,0:T(8,128)(2,1)}, u32[]{:S(2)}) copy-start(bf16[1024,1024]{1,0:T(8,128)(2,1)} %param.12) | copy-start | bytes 6291460
  149.8 104.0 %reduce-scatter.13.cloned.1.call-start = ((), (), s32[]{:S(2)}) async-start(), calls=%async_computation.11 | async-start | bytes 2359296
  156.9 167.7 %reduce-scatter.9.cloned.1.call-start = ((), (), s32[]{:S(2)}) async-start(), calls=%async_computation.9 | async-start | bytes 2359296 | tf_op jit(solution)/shard_map/reduce_scatter | solution.py:130
  159.1 300.9 %reduce-scatter.11.cloned.1.call-start = ((), (), s32[]{:S(2)}) async-start(), calls=%async_computation.10 | async-start | bytes 8257536 | tf_op jit(solution)/shard_map/reduce_scatter | solution.py:84
  164.2 17.5 %copy-start.2 = (bf16[16,1024]{1,0:T(8,128)(2,1)S(1)}, bf16[16,1024]{1,0:T(8,128)(2,1)}, u32[]{:S(2)}) copy-start(bf16[16,1024]{1,0:T(8,128)(2,1)} %param.11) | copy-start | bytes 98308
  164.2 18.4 %copy-start.4 = (bf16[16,1024]{1,0:T(8,128)(2,1)S(1)}, bf16[16,1024]{1,0:T(8,128)(2,1)}, u32[]{:S(2)}) copy-start(bf16[16,1024]{1,0:T(8,128)(2,1)} %reduce-scatter.7.cloned.1.call-done) | copy-start | bytes 98308
Sparse Core Ops, SparseCore 0:
  17.7 33.3 all-reduce.2
  121.9 18.7 reduce-scatter.6
  149.9 31.7 all-reduce.4
  185.1 68.6 reduce-scatter.12
  257.2 67.3 reduce-scatter.8
  328.0 131.9 reduce-scatter.10
where the time goes:
time: 471 us; the launch traced here: 470 us
  waiting for transfers between devices  355 us (75%)
  matrix products  28.4 us (6%)
  local copies, waits for them, and re-layouts  22.6 us (5%)
  other arithmetic  19.4 us (4%)
  starting transfers between devices  17.1 us (4%)
  between operations  14.4 us (3%)
  blocking collectives  12.8 us (3%)
    reduce_scatter x1, waiting for transfers between devices, local(): lax.psum_scatter((jnp.einsum('rk,rc->kc', tap_rows, coarse_grad, preferre...  134 us
    unnamed x7, waiting for transfers between devices  69.8 us
    reduce_scatter x1, waiting for transfers between devices, local(): lax.psum_scatter((jnp.einsum('rd,rf->df', normed, pre_grad, preferred_ele...  68.8 us
    psum x2, waiting for transfers between devices, tp_sums(): return lax.psum(terms.astype(jnp.bfloat16), 'tp').astype(jnp.float32)  49.2 us
    reduce_scatter x1, waiting for transfers between devices, local(): lax.psum_scatter(partial_value.astype(jnp.bfloat16), 'tp', scatter_dimens...  18.8 us
    all_gather x2, blocking collectives, tp_rows(): return lax.all_gather(pieces, 'tp', axis=0, tiled=True)  12.8 us
  transfers between devices with their start and end apart: 12, of which 11 were waited for; matrix products, arithmetic and copies ran while one was open for 5% of the time, Pallas kernels for 0%

commit v1 on v0

--- a/solution.py
+++ b/solution.py
@@ -32,7 +32,7 @@
 
 
 def tp_sums(terms):
-    return lax.psum(terms.astype(jnp.bfloat16), "tp").astype(jnp.float32)
+    return jnp.sum(lax.all_gather(terms.astype(jnp.bfloat16), "tp"), axis=0).astype(jnp.float32)
 
 
 def tile_margin(tile_data):

time: 471 us -> 412 us (0.87)
  waiting for transfers between devices: 355 us -> 282 us
  blocking collectives: 12.8 us -> 27.5 us
    psum x2 -> x0, waiting for transfers between devices: 49.2 us -> none  [tp_sums(): return lax.psum(terms.astype(jnp.bfloat16), 'tp').astype(jnp.float32)]
    unnamed x7 -> x5, waiting for transfers between devices: 69.8 us -> 46.4 us
    all_gather x0 -> x2, blocking collectives: none -> 14.8 us  [tp_sums(): lax.all_gather(terms.astype(jnp.bfloat16), 'tp')]
  transfers between devices with their start and end apart: 12 -> 10, of which waited for: 11 -> 8; matrix products, arithmetic and copies ran while one was open for 5% -> 5% of each run, Pallas kernels for 0% -> 0%
where the time goes in v1:
time: 412 us; the launch traced here: 411 us
  waiting for transfers between devices  282 us (68%)
  matrix products  27.6 us (7%)
  blocking collectives  27.5 us (7%)
  local copies, waits for them, and re-layouts  24.8 us (6%)
  other arithmetic  17.2 us (4%)
  starting transfers between devices  17.1 us (4%)
  between operations  14.1 us (3%)
    reduce_scatter x1, waiting for transfers between devices, local(): lax.psum_scatter((jnp.einsum('rk,rc->kc', tap_rows, coarse_grad, preferre...  134 us
    reduce_scatter x1, waiting for transfers between devices, local(): lax.psum_scatter((jnp.einsum('rd,rf->df', normed, pre_grad, preferred_ele...  68.9 us
    unnamed x5, waiting for transfers between devices  46.4 us
    reduce_scatter x1, waiting for transfers between devices, local(): lax.psum_scatter(partial_value.astype(jnp.bfloat16), 'tp', scatter_dimens...  19 us
    all_gather x2, blocking collectives, tp_sums(): lax.all_gather(terms.astype(jnp.bfloat16), 'tp')  14.8 us
    all_gather x2, blocking collectives, tp_rows(): return lax.all_gather(pieces, 'tp', axis=0, tiled=True)  12.7 us
  transfers between devices with their start and end apart: 10, of which 8 were waited for; matrix products, arithmetic and copies ran while one was open for 5% of the time, Pallas kernels for 0%

profile of v1, /device:TPU:0, one launch (start us, length us, event | category | flops | bytes accessed | tf_op | source)
XLA Modules:
  0.0 410.5 jit_solution(14272995744859670024)
XLA Ops:
  7.2 6.9 %all_gather.18 = bf16[64,1024]{1,0:T(8,128)(2,1)S(1)} all-gather(bf16[16,1024]{1,0:T(8,128)(2,1)} %param.11), channel_id=1, replica_groups=mesh['tile'=8,'tp'=4] {'tp'}, dimensions={0}, use_global_device_ids=true | all-gather | bytes 163840 | tf_op jit(solution)/shard_map/all_gather | solution.py:31
  14.1 0.1 fusion.1
  14.2 2.1 fusion.23
  16.3 0.7 copy-done.2
  17.0 0.5 convolution_convert_fusion.1
  17.5 7.6 %all-gather = bf16[256,1024]{1,0:T(8,128)(2,1)S(1)} all-gather(bf16[64,1024]{1,0:T(8,128)(2,1)S(1)} %convolution_convert_fusion.1), channel_id=2, replica_groups=mesh['tile'=8,'tp'=4] {'tp'}, dimensions={0}, use_global_device_ids=true | all-gather | bytes 655360 | tf_op jit(solution)/shard_map/all_gather | solution.py:35
  25.1 0.1 reduce_sum.43
  25.2 3.5 collective-permute-start
  28.7 1.3 collective-permute-start.1
  30.0 0.1 copy.28
  30.1 0.1 reshape.168
  30.3 0.1 copy.27
  30.5 4.0 collective-permute-done.1
  34.5 0.1 maximum_maximum_fusion
  34.6 2.7 gather_fusion
  37.3 2.2 reshape.167
  39.5 1.4 broadcast_select_fusion
  40.9 0.6 copy.36
  41.6 5.1 %convolution_convert_fusion.2 = bf16[64,512]{1,0:T(8,128)(2,1)} fusion(bf16[64,7168]{1,0:T(8,128)(2,1)S(1)} %bitcast.57, bf16[7168,512]{1,0:T(8,128)(2,1)} %param.14), kind=kOutput, calls=%fused_computation.11 | convolution fusion | flops 469794816 | bytes 8323072 | tf_op jit(solution)/shard_map/dot_general | solution.py:70
  46.7 3.3 all-to-all-start
  50.0 0.1 copy.31
  50.1 0.1 reshape.161
  50.2 1.2 scatter_custom_fusion
  51.4 2.7 all-to-all-done
  54.0 1.2 copy.29
  55.2 1.5 copy.30
  56.9 1.1 copy.32
  57.9 1.8 copy.33
  59.8 3.3 all-to-all-start.1
  63.1 4.0 all-to-all-done.1
  67.2 6.6 %fusion.29 = f32[64,7168]{1,0:T(8,128)} fusion(bf16[64,512]{1,0:T(8,128)(2,1)S(1)} %bitcast.65, bf16[7168,512]{1,0:T(8,128)(2,1)} %param.14), kind=kOutput, calls=%fused_computation.66 | convolution fusion | flops 469762048 | bytes 9240576 | tf_op jit(solution)/shard_map/dot_general | solution.py:93
  73.8 2.7 reshape.194
  76.5 5.9 %scatter_custom_fusion.1 = f32[97,1024]{1,0:T(8,128)} fusion(s32[448]{0:T(512)S(1)} %bitcast.69, f32[448,1024]{1,0:T(8,128)} %reshape.194, f32[]{:T(128)} %constant.112.clone.1), kind=kCustom, calls=%fused_computation.22 | custom fusion | flops 458752 | bytes 397824 | tf_op jit(solution)/shard_map/scatter-add | solution.py:98
  82.4 1.0 convert.11
  83.4 4.4 %collective-permute-start.2 = (bf16[16,1024]{1,0:T(8,128)(2,1)S(1)}, bf16[16,1024]{1,0:T(8,128)(2,1)S(1)}, u32[]{:S(2)}, u32[]{:S(2)}) collective-permute-start(bf16[16,1024]{1,0:T(8,128)(2,1)S(1)} %get-tuple-element.29), channel_id=1, source_target_pairs={{0,4},{4,8},{8,12},{12,16},{16,20},{20,24},{24,28},{1,5},{5,9},{9,... | collective-permute-start | bytes 98312 | tf_op jit(solution)/shard_map/ppermute | solution.py:19
  87.8 1.3 collective-permute-start.3
  89.1 1.0 slice.79
  90.1 3.5 collective-permute-done.3
  93.6 0.8 fusion.21
  94.5 0.7 convert_element_type.103
  95.2 19.0 %reduce-scatter.7.cloned.1.call-done = bf16[16,1024]{1,0:T(8,128)(2,1)} async-done(((bf16[64,1024]{1,0:T(8,128)(2,1)}), bf16[16,1024]{1,0:T(8,128)(2,1)}) %reduce-scatter.7.cloned.1.call-update) | async-done | bytes 32784 | tf_op jit(solution)/shard_map/reduce_scatter | solution.py:107
  114.2 5.8 %all_gather.21 = bf16[64,1024]{1,0:T(8,128)(2,1)S(1)} all-gather(bf16[16,1024]{1,0:T(8,128)(2,1)} %reduce-scatter.7.cloned.1.call-done), channel_id=1, replica_groups=mesh['tile'=8,'tp'=4] {'tp'}, dimensions={0}, use_global_device_ids=true | all-gather | bytes 163840 | tf_op jit(solution)/shard_map/all_gather | solution.py:31
  120.0 0.7 copy-done.5
  120.7 2.1 multiply_convert_fusion.1
  122.8 4.0 copy.34
  126.8 0.8 copy-done.6
  127.7 1.7 fusion
  129.4 2.1 multiply_convert_fusion.2
  131.6 5.1 %multiply_convert_fusion = bf16[7168,512]{1,0:T(8,128)(2,1)} fusion(bf16[64,7168]{1,0:T(8,128)(2,1)S(1)} %bitcast.58, bf16[64,512]{1,0:T(8,128)(2,1)S(1)} %bitcast.66), kind=kOutput, calls=%fused_computation.4 | convolution fusion | flops 477102080 | bytes 8323072 | tf_op jit(solution)/shard_map/rk,rc->kc/dot_general | solution.py:86
  136.7 0.1 dynamic-slice.19
  136.8 0.7 gather_fusion.1
  137.5 0.7 broadcast_select_fusion.1
  138.2 2.4 convolution_convert_fusion
  140.5 7.3 %all-gather.1 = bf16[256,1024]{1,0:T(8,128)(2,1)S(1)} all-gather(bf16[64,1024]{1,0:T(8,128)(2,1)S(1)} %convolution_convert_fusion), channel_id=3, replica_groups=mesh['tile'=8,'tp'=4] {'tp'}, dimensions={0}, use_global_device_ids=true | all-gather | bytes 655360 | tf_op jit(solution)/shard_map/all_gather | solution.py:35
  147.8 0.1 reduce_sum.44
  147.9 0.1 fusion.19
  148.0 0.7 fusion.15
  148.8 46.3 %reduce-scatter.13.cloned.1.call-done = bf16[128,1024]{1,0:T(8,128)(2,1)} async-done(((bf16[1024,1024]{1,0:T(8,128)(2,1)}), bf16[128,1024]{1,0:T(8,128)(2,1)}) %reduce-scatter.13.cloned.1.call-update) | async-done | bytes 262160
  195.1 1.1 copy.35
  196.2 0.8 convert_element_type.112
  197.0 68.9 %reduce-scatter.9.cloned.1.call-done = bf16[128,1024]{1,0:T(8,128)(2,1)} async-done(((bf16[1024,1024]{1,0:T(8,128)(2,1)}), bf16[128,1024]{1,0:T(8,128)(2,1)}) %reduce-scatter.9.cloned.1.call-update) | async-done | bytes 262160 | tf_op jit(solution)/shard_map/reduce_scatter | solution.py:130
  266.0 1.8 convert_element_type.110
  267.8 133.6 %reduce-scatter.11.cloned.1.call-done = bf16[896,512]{1,0:T(8,128)(2,1)} async-done(((bf16[7168,512]{1,0:T(8,128)(2,1)}), bf16[896,512]{1,0:T(8,128)(2,1)}) %reduce-scatter.11.cloned.1.call-update) | async-done | bytes 917520 | tf_op jit(solution)/shard_map/reduce_scatter | solution.py:84
  401.3 2.7 convert_element_type.114
  (41 shorter events, 0.6 us)
Async XLA Ops:
  7.2 9.9 %copy-start = (bf16[1024,1024]{1,0:T(8,128)(2,1)S(1)}, bf16[1024,1024]{1,0:T(8,128)(2,1)}, u32[]{:S(2)}) copy-start(bf16[1024,1024]{1,0:T(8,128)(2,1)} %param.13) | copy-start | bytes 6291460
  16.3 0.7 copy-start.2
  17.0 13.0 %copy-start.7 = (s32[64,7]{0,1:T(8,128)S(1)}, s32[64,7]{0,1:T(8,128)}, u32[]{:S(2)}) copy-start(s32[64,7]{0,1:T(8,128)} %param.15) | copy-start | bytes 5380
  25.2 5.3 %collective-permute-start = (bf16[16,1024]{1,0:T(8,128)(2,1)S(1)}, bf16[16,1024]{1,0:T(8,128)(2,1)S(1)}, u32[]{:S(2)}, u32[]{:S(2)}) collective-permute-start(bf16[16,1024]{1,0:T(8,128)(2,1)S(1)} %get-tuple-element.33), channel_id=1, source_target_pairs={{0,4},{4,8},{8,12},{12,16},{16,20},{20,24},{24,28},{1,5},{5,9},{9,... | collective-permute-start | bytes 98312 | tf_op jit(solution)/shard_map/ppermute | solution.py:19
  28.7 5.8 %collective-permute-start.1 = (bf16[16,1024]{1,0:T(8,128)(2,1)S(1)}, bf16[16,1024]{1,0:T(8,128)(2,1)S(1)}, u32[]{:S(2)}, u32[]{:S(2)}) collective-permute-start(bf16[16,1024]{1,0:T(8,128)(2,1)S(1)} %get-tuple-element.34), channel_id=1, source_target_pairs={{4,0},{8,4},{12,8},{16,12},{20,16},{24,20},{28,24},{5,1},{9,5},{13... | collective-permute-start | bytes 98312 | tf_op jit(solution)/shard_map/ppermute | solution.py:20
  41.5 8.4 %copy-start.8 = (s32[64]{0:T(128)S(1)}, s32[64]{0:T(128)}, u32[]{:S(2)}) copy-start(s32[64]{0:T(128)} %param.16) | copy-start | bytes 772
  46.7 7.4 %all-to-all-start = ((bf16[4,16,512]{2,1,0:T(8,128)(2,1)}), bf16[4,16,512]{2,1,0:T(8,128)(2,1)S(1)}, u32[]{:S(2)}, u32[]{:S(2)}) async-start(bf16[4,16,512]{2,1,0:T(8,128)(2,1)} %bitcast.1), calls=%async_computation | async-start | bytes 131072 | tf_op jit(solution)/shard_map/all_to_all | solution.py:43
  59.8 7.4 %all-to-all-start.1 = ((bf16[4,16,512]{2,1,0:T(8,128)(2,1)}), bf16[4,16,512]{2,1,0:T(8,128)(2,1)S(1)}, u32[]{:S(2)}, u32[]{:S(2)}) async-start(bf16[4,16,512]{2,1,0:T(8,128)(2,1)} %copy.33), calls=%async_computation.1 | async-start | bytes 131072 | tf_op jit(solution)/shard_map/all_to_all | solution.py:43
  63.1 51.1 %reduce-scatter.7.cloned.1.call-start = ((), (), s32[]{:S(2)}) async-start(), calls=%async_computation.6 | async-start | bytes 163840 | tf_op jit(solution)/shard_map/reduce_scatter | solution.py:107
  76.5 44.2 %copy-start.3 = (f32[64,1024]{1,0:T(8,128)S(1)}, f32[64,1024]{1,0:T(8,128)}, u32[]{:S(2)}) copy-start(f32[64,1024]{1,0:T(8,128)} %copy-done.2) | copy-start | bytes 786436
  83.4 6.6 %collective-permute-start.2 = (bf16[16,1024]{1,0:T(8,128)(2,1)S(1)}, bf16[16,1024]{1,0:T(8,128)(2,1)S(1)}, u32[]{:S(2)}, u32[]{:S(2)}) collective-permute-start(bf16[16,1024]{1,0:T(8,128)(2,1)S(1)} %get-tuple-element.29), channel_id=1, source_target_pairs={{0,4},{4,8},{8,12},{12,16},{16,20},{20,24},{24,28},{1,5},{5,9},{9,... | collective-permute-start | bytes 98312 | tf_op jit(solution)/shard_map/ppermute | solution.py:19
  87.8 5.8 %collective-permute-start.3 = (bf16[16,1024]{1,0:T(8,128)(2,1)S(1)}, bf16[16,1024]{1,0:T(8,128)(2,1)S(1)}, u32[]{:S(2)}, u32[]{:S(2)}) collective-permute-start(bf16[16,1024]{1,0:T(8,128)(2,1)S(1)} %get-tuple-element.30), channel_id=1, source_target_pairs={{4,0},{8,4},{12,8},{16,12},{20,16},{24,20},{28,24},{5,1},{9,5},{13... | collective-permute-start | bytes 98312 | tf_op jit(solution)/shard_map/ppermute | solution.py:20
  95.2 99.9 %reduce-scatter.13.cloned.1.call-start = ((), (), s32[]{:S(2)}) async-start(), calls=%async_computation.9 | async-start | bytes 2359296
  120.0 0.7 copy-start.5
  126.8 0.9 copy-start.6
  126.8 139.2 %reduce-scatter.9.cloned.1.call-start = ((), (), s32[]{:S(2)}) async-start(), calls=%async_computation.7 | async-start | bytes 2359296 | tf_op jit(solution)/shard_map/reduce_scatter | solution.py:130
  131.5 269.8 %reduce-scatter.11.cloned.1.call-start = ((), (), s32[]{:S(2)}) async-start(), calls=%async_computation.8 | async-start | bytes 8257536 | tf_op jit(solution)/shard_map/reduce_scatter | solution.py:84
  136.7 11.2 %copy-start.1 = (bf16[16,1024]{1,0:T(8,128)(2,1)S(1)}, bf16[16,1024]{1,0:T(8,128)(2,1)}, u32[]{:S(2)}) copy-start(bf16[16,1024]{1,0:T(8,128)(2,1)} %param.11) | copy-start | bytes 98308
  136.8 11.3 %copy-start.4 = (bf16[16,1024]{1,0:T(8,128)(2,1)S(1)}, bf16[16,1024]{1,0:T(8,128)(2,1)}, u32[]{:S(2)}) copy-start(bf16[16,1024]{1,0:T(8,128)(2,1)} %reduce-scatter.7.cloned.1.call-done) | copy-start | bytes 98308
Sparse Core Ops, SparseCore 0:
  95.3 18.9 reduce-scatter.6
  126.9 68.1 reduce-scatter.12
  198.6 67.3 reduce-scatter.8
  269.4 131.8 reduce-scatter.10
